TPU v7x, 256 devices: a whole 4x4x8 slice. The times are simulated.
256 devices in a mesh: seq: 8 (over z_hi, core), req: 32 (over x, z_lo, y).
Axes of the slice: x: 4, y: 4, z: 8 (z_hi: 4, z_lo: 2; z = z_hi * 2 + z_lo), core: 2. Of those that a mesh axis runs over, the one named last changes fastest.
Arguments:
- inputs: bfloat16 [32, 16, 4, 1536], P('req', 'seq'), may hold values from -6 to 6
- parents: int32 [32, 4, 16], P('req'), may hold values from 0 to 15
- block_len: int32 [32, 128], P('req', 'seq'), may hold values from 0 to 128, as said below
- prompt_key_cache: bfloat16 [32, 16384, 512], P('req', 'seq'), may hold values from -230 to 230
- prompt_value_cache: bfloat16 [32, 16384, 512], P('req', 'seq'), may hold values from -6 to 6
- generated_key_cache: bfloat16 [32, 16, 16, 512], P('req', 'seq'), may hold values from -6 to 6
- generated_value_cache: bfloat16 [32, 16, 16, 512], P('req', 'seq'), may hold values from -6 to 6
- gain_attn: float32 [1536], replicated, may hold values from 0.1 to 1.9
- gain_moe: float32 [1536], replicated, may hold values from 0.1 to 1.9
- w_query: bfloat16 [1536, 1536], P(None, 'seq'), may hold values from -0.15625 to 0.15625
- key_projection_weight: bfloat16 [1536, 512], P(None, 'seq'), may hold values from -0.15625 to 0.15625
- value_projection_weight: bfloat16 [1536, 512], P(None, 'seq'), may hold values from -0.15625 to 0.15625
- w_output: bfloat16 [1536, 1536], P('seq'), may hold values from -0.15625 to 0.15625
- w_in: bfloat16 [32, 1536, 1024], P('req'), may hold values from -0.15625 to 0.15625
- w_out: bfloat16 [32, 512, 1536], P('req'), may hold values from -0.25 to 0.25
- routes: int32 [32, 16, 4, 8], P('req', 'seq'), may hold values from 0 to 31, all different within a row; in each aligned block of 8 rows (0 to 7, 8 to 15, ..., all dimensions but the last counted through in order) at most 4 rows name the same one
- gate_weights: float32 [32, 16, 4, 8], P('req', 'seq'), may hold values from 0.05 to 1
Outputs:
- mixed: bfloat16 [32, 16, 4, 1536], P('req', 'seq')
- final_k: bfloat16 [32, 16, 20, 512], P('req', 'seq')
- final_v: bfloat16 [32, 16, 20, 512], P('req', 'seq')
Inputs may be any that keep to these rules, and one draw needn't show every extreme that they name: block_len[r, j] is the number of live positions at the start of block j of request r; 0 marks an empty block; the first block of every request is full. `routes`: among the rows of one device (its 2 beams over all 4 steps, in the order beam then step) no expert is named more than 4 times.
All inputs are finite; a program needn't handle non-finite values.
Results may differ from a plain program's by a relative error of at most 0.025.
Values may be sent and summed in bfloat16 or wider, within the bound.
No kernel may reach another device: no remote copies, remote signals or barrier semaphores. Data moves between devices by JAX's collectives and lax.ppermute only.
A program may use at most 128 MiB of HBM per device.

v0:
```python
from functools import reduce
import jax
import jax.numpy as jnp
from jax import lax
from jax.sharding import PartitionSpec as P

QUERY_HEADS = 24
HEAD_SIZE = 64
BLK = 128
EPSILON = 1e-05
ROPE_BASE = 10000.0
NEGATIVE_FILL = -1e30
SCORE_SCALE = 0.125


def merged(x, axis, join):
    gathered = jax.tree.map(
        lambda a, kind: lax.all_gather(a.astype(kind), axis),
        x,
        jax.tree.map(lambda a: jnp.bfloat16 if a.dtype == jnp.float32 else a.dtype, x),
    )

    def take(source):
        return jax.tree.map(
            lambda a, own: lax.dynamic_index_in_dim(a, source, 0, False).astype(own.dtype),
            gathered,
            x,
        )

    return lax.fori_loop(
        1, lax.axis_size(axis), lambda source, state: join(state, take(source)), take(0)
    )


def rms_scale(values, gain_vector):
    values = values.astype(jnp.float32)
    mean_sq = jnp.mean(values * values, axis=-1, keepdims=True)
    return values * lax.rsqrt(mean_sq + EPSILON) * gain_vector


def apply_rotary(values, token_positions, head_dim):
    lead_shape = values.shape[:-1]
    head_count = values.shape[-1] // head_dim
    shaped = values.reshape(lead_shape + (head_count, head_dim))
    half_dim = head_dim // 2
    frequency = ROPE_BASE ** (-(jnp.arange(half_dim, dtype=jnp.float32) * 2.0 / head_dim))
    angles = token_positions[:, None] * frequency[None, :]
    cosine = jnp.cos(angles)[None, :, None, :]
    sine_part = jnp.sin(angles)[None, :, None, :]
    first_half = shaped[..., :half_dim]
    second = shaped[..., half_dim:]
    turned = jnp.concatenate(
        [first_half * cosine - second * sine_part, second * cosine + first_half * sine_part],
        axis=-1,
    )
    return turned.reshape(values.shape)


def project(row_block, weight):
    flattened_rows = row_block.reshape(-1, row_block.shape[-1])
    result = jnp.dot(flattened_rows, weight, preferred_element_type=jnp.float32)
    return result.reshape(row_block.shape[:-1] + (weight.shape[1],))


def local_partial(decode_query_step, pieces):
    scored = []
    for key_rows, values, live in pieces:
        shaped_keys = key_rows.reshape(
            key_rows.shape[0], decode_query_step.shape[1], decode_query_step.shape[3]
        )
        scores = (
            jnp.einsum(
                "bgjd,kgd->bgjk", decode_query_step, shaped_keys, preferred_element_type=jnp.float32
            )
            * SCORE_SCALE
        )
        mask = live[:, None, None, :]
        scored.append(
            (jnp.where(mask, scores, NEGATIVE_FILL), mask, values.reshape(shaped_keys.shape))
        )
    row_max = reduce(jnp.maximum, [jnp.max(entry[0], axis=-1) for entry in scored])
    denominator = jnp.zeros(row_max.shape, jnp.float32)
    numerator = jnp.zeros(row_max.shape + (decode_query_step.shape[3],), jnp.float32)
    for entry in scored:
        weights = jnp.where(entry[1], jnp.exp(entry[0] - row_max[..., None]), 0.0)
        denominator = denominator + jnp.sum(weights, axis=-1)
        numerator = numerator + jnp.einsum(
            "bgjk,kgd->bgjd",
            weights.astype(jnp.bfloat16),
            entry[2],
            preferred_element_type=jnp.float32,
        )
    return (row_max, denominator, numerator)


def join_partials(first_part, second_part):
    row_max = jnp.maximum(first_part[0], second_part[0])
    first_scale = jnp.exp(first_part[0] - row_max)
    second_scale = jnp.exp(second_part[0] - row_max)
    denominator = first_scale * first_part[1] + second_scale * second_part[1]
    numerator = first_scale[..., None] * first_part[2] + second_scale[..., None] * second_part[2]
    return (row_max, denominator, numerator)


def expert_block(received, w_in, w_out):
    half_dim = w_out.shape[1]
    projected = jnp.einsum("nesd,edf->nesf", received, w_in, preferred_element_type=jnp.float32)
    activation = (jax.nn.silu(projected[..., :half_dim]) * projected[..., half_dim:]).astype(
        jnp.bfloat16
    )
    return jnp.einsum(
        "nesf,efd->nesd", activation, w_out, preferred_element_type=jnp.float32
    ).astype(jnp.bfloat16)


def route_rows(expert_in, route_ids, pair_weights, capacity, dev_count, experts_all, send_rows):
    row_count, top_count = route_ids.shape
    pair_count = row_count * top_count
    chosen = route_ids.reshape(pair_count)
    pair_index = jnp.arange(pair_count, dtype=jnp.int32)
    before = (chosen[:, None] == chosen[None, :]) & (pair_index[None, :] < pair_index[:, None])
    slot_rank = jnp.sum(before.astype(jnp.int32), axis=1)
    slot_index = chosen * capacity + slot_rank
    slot_table = (
        slot_index[:, None] == jnp.arange(experts_all * capacity, dtype=jnp.int32)[None, :]
    ).astype(jnp.float32)
    row_table = (
        (pair_index // top_count)[:, None] == jnp.arange(row_count, dtype=jnp.int32)[None, :]
    ).astype(jnp.float32)
    placing = jnp.dot(slot_table.T, row_table, precision=lax.Precision.HIGHEST)
    buffer = jnp.dot(
        placing.astype(jnp.bfloat16), expert_in, preferred_element_type=jnp.float32
    ).astype(jnp.bfloat16)
    buffer = buffer.reshape(dev_count, experts_all // dev_count, capacity, expert_in.shape[1])
    returned = send_rows(buffer).reshape(experts_all * capacity, expert_in.shape[1])
    mixing = jnp.dot(
        row_table.T * pair_weights.reshape(pair_count)[None, :],
        slot_table,
        precision=lax.Precision.HIGHEST,
    )
    return jnp.dot(mixing, returned.astype(jnp.float32), precision=lax.Precision.HIGHEST)


def local(
    inputs,
    parents,
    block_len,
    prompt_key_cache,
    prompt_value_cache,
    generated_key_cache,
    generated_value_cache,
    gain_attn,
    gain_moe,
    w_query,
    key_projection_weight,
    value_projection_weight,
    w_output,
    w_in,
    w_out,
    routes,
    gate_weights,
):
    rows_here = inputs.shape[1]
    step_count = inputs.shape[2]
    model_width = inputs.shape[3]
    seq_count = lax.axis_size("seq")
    my_seq = lax.axis_index("seq")
    req_count = lax.axis_size("req")
    experts_all = w_in.shape[0] * req_count
    beam_count = rows_here * seq_count
    prefix_len = prompt_key_cache.shape[1]
    tail_len = generated_key_cache.shape[2]
    kv_width = prompt_key_cache.shape[2]
    kv_heads = kv_width // HEAD_SIZE
    group_size = QUERY_HEADS // kv_heads
    token_positions = jnp.arange(step_count, dtype=jnp.float32) + (
        prefix_len * seq_count + tail_len
    )
    normed = rms_scale(inputs[0], gain_attn).astype(jnp.bfloat16)
    normed_all = lax.all_gather(normed, "seq", axis=0, tiled=True)
    query_rows = apply_rotary(project(normed_all, w_query), token_positions, HEAD_SIZE).astype(
        jnp.bfloat16
    )
    updated_keys = apply_rotary(
        project(normed_all, key_projection_weight), token_positions, HEAD_SIZE
    ).astype(jnp.bfloat16)
    updated_values = project(normed_all, value_projection_weight).astype(jnp.bfloat16)
    queries_all = lax.all_gather(query_rows, "seq", axis=2, tiled=True)
    entry_k, entry_v = (
        lax.all_to_all(updated_keys, "seq", split_axis=0, concat_axis=2, tiled=True),
        lax.all_to_all(updated_values, "seq", split_axis=0, concat_axis=2, tiled=True),
    )
    block_count = block_len.shape[1]
    prefix_live = (jnp.arange(BLK, dtype=jnp.int32)[None, :] < block_len[0][:, None]).reshape(
        1, block_count * BLK
    )
    own_ids = my_seq * rows_here + jnp.arange(rows_here, dtype=jnp.int32)
    beam_ids = jnp.arange(beam_count, dtype=jnp.int32)
    tail_owner = (own_ids[:, None] + jnp.zeros((1, tail_len), jnp.int32)).reshape(
        rows_here * tail_len
    )
    fresh_owner = (own_ids[:, None] + jnp.zeros((1, step_count), jnp.int32)).reshape(
        rows_here * step_count
    )
    fresh_step = (
        jnp.zeros((rows_here, 1), jnp.int32) + jnp.arange(step_count, dtype=jnp.int32)[None, :]
    ).reshape(rows_here * step_count)
    my_parents = lax.dynamic_slice_in_dim(parents[0], my_seq * rows_here, rows_here, 1)
    head_width = w_output.shape[0]

    def send_batch(buffer):
        return lax.all_to_all(
            expert_block(
                lax.all_to_all(buffer, "req", split_axis=0, concat_axis=0, tiled=True), w_in, w_out
            ),
            "req",
            split_axis=0,
            concat_axis=0,
            tiled=True,
        )

    beam_key_cache = generated_key_cache[0]
    beam_value_cache = generated_value_cache[0]
    newest_key = jnp.zeros((rows_here, step_count, kv_width), jnp.bfloat16)
    newest_value = jnp.zeros((rows_here, step_count, kv_width), jnp.bfloat16)
    hidden_rows = []
    for decode_step_index in range(step_count):
        chosen_rows = my_parents[decode_step_index]
        received = (
            lax.all_gather(beam_key_cache, "seq", axis=0, tiled=True),
            lax.all_gather(beam_value_cache, "seq", axis=0, tiled=True),
            lax.all_gather(newest_key, "seq", axis=0, tiled=True),
            lax.all_gather(newest_value, "seq", axis=0, tiled=True),
        )
        beam_key_cache = jnp.take(received[0], chosen_rows, axis=0)
        beam_value_cache = jnp.take(received[1], chosen_rows, axis=0)
        newest_key = jnp.take(received[2], chosen_rows, axis=0)
        newest_value = jnp.take(received[3], chosen_rows, axis=0)
        newest_key = newest_key.at[:, decode_step_index].set(entry_k[:, decode_step_index])
        newest_value = newest_value.at[:, decode_step_index].set(entry_v[:, decode_step_index])
        decode_query_step = queries_all[:, decode_step_index].reshape(
            beam_count, kv_heads, group_size, HEAD_SIZE
        )
        tail_live = beam_ids[:, None] == tail_owner[None, :]
        fresh_live = (beam_ids[:, None] == fresh_owner[None, :]) & (
            fresh_step[None, :] <= decode_step_index
        )
        pieces = [
            (prompt_key_cache[0], prompt_value_cache[0], prefix_live),
            (
                beam_key_cache.reshape(rows_here * tail_len, kv_width),
                beam_value_cache.reshape(rows_here * tail_len, kv_width),
                tail_live,
            ),
            (
                newest_key.reshape(rows_here * step_count, kv_width),
                newest_value.reshape(rows_here * step_count, kv_width),
                fresh_live,
            ),
        ]
        partial_state = local_partial(decode_query_step, pieces)
        row_max, denominator, numerator = merged(partial_state, "seq", join_partials)
        attended_heads = (
            (numerator / denominator[..., None])
            .reshape(beam_count, QUERY_HEADS * HEAD_SIZE)
            .astype(jnp.bfloat16)
        )
        own_heads = lax.dynamic_slice_in_dim(attended_heads, my_seq * head_width, head_width, 1)
        attended = lax.psum_scatter(
            jnp.dot(own_heads, w_output, preferred_element_type=jnp.float32).astype(jnp.bfloat16),
            "seq",
            scatter_dimension=0,
            tiled=True,
        ).astype(jnp.float32)
        hidden = inputs[0][:, decode_step_index].astype(jnp.float32) + attended
        hidden_rows.append(hidden)
    stacked = jnp.stack(hidden_rows, axis=1).reshape(rows_here * step_count, model_width)
    expert_in = rms_scale(stacked, gain_moe).astype(jnp.bfloat16)
    capacity = 2 * rows_here * step_count * routes.shape[3] // experts_all
    route_ids = routes[0].reshape(rows_here * step_count, routes.shape[3])
    pair_weights = gate_weights[0].reshape(rows_here * step_count, routes.shape[3])
    summed = route_rows(
        expert_in, route_ids, pair_weights, capacity, req_count, experts_all, send_batch
    )
    mixed = (stacked + summed).astype(jnp.bfloat16).reshape(rows_here, step_count, model_width)
    final_k = jnp.concatenate([beam_key_cache, newest_key], axis=1)
    final_v = jnp.concatenate([beam_value_cache, newest_value], axis=1)
    return (mixed[None], final_k[None], final_v[None])


def solution(mesh):
    placed = (
        P("req", "seq", None, None),
        P("req", None, None),
        P("req", "seq"),
        P("req", "seq", None),
        P("req", "seq", None),
        P("req", "seq", None, None),
        P("req", "seq", None, None),
        P(),
        P(),
        P(None, "seq"),
        P(None, "seq"),
        P(None, "seq"),
        P("seq", None),
        P("req", None, None),
        P("req", None, None),
        P("req", "seq", None, None),
        P("req", "seq", None, None),
    )
    return jax.shard_map(
        local,
        mesh=mesh,
        in_specs=placed,
        out_specs=(
            P("req", "seq", None, None),
            P("req", "seq", None, None),
            P("req", "seq", None, None),
        ),
        check_vma=False,
    )
```

profile of v0, /device:TPU:8, one launch (start us, length us, event | category | flops | bytes accessed | tf_op | source)
XLA Modules:
  0.0 895.3 jit_solution(18292231915327274517)
XLA Ops:
  9.3 18.2 %all_gather.108 = bf16[16,4,1536]{2,1,0:T(4,128)(2,1)S(1)} all-gather(bf16[2,4,1536]{2,1,0:T(4,128)(2,1)S(1)} %fusion.149), channel_id=1, replica_groups=mesh['seq'=8,'req'=32] {'seq'}, dimensions={0}, use_global_device_ids=true | all-gather | bytes 221184 | tf_op jit(solution)/shard_map/all_gather | solution.py:180
  38.5 18.3 %all-gather.3 = bf16[1,16,16,512]{3,2,0,1:T(8,128)(2,1)} all-gather(bf16[1,2,16,512]{3,2,0,1:T(8,128)(2,1)} %bitcast.429), channel_id=5, replica_groups=mesh['seq'=8,'req'=32] {'seq'}, dimensions={1}, use_global_device_ids=true | all-gather | bytes 294912 | tf_op jit(solution)/shard_map/all_gather | solution.py:231
  56.8 16.0 %all-gather = bf16[1,16,16,512]{3,2,0,1:T(8,128)(2,1)} all-gather(bf16[1,2,16,512]{3,2,0,1:T(8,128)(2,1)} %bitcast.430), channel_id=2, replica_groups=mesh['seq'=8,'req'=32] {'seq'}, dimensions={1}, use_global_device_ids=true | all-gather | bytes 294912 | tf_op jit(solution)/shard_map/all_gather | solution.py:230
  75.9 15.7 %all_gather.117 = bf16[16,16,512]{2,1,0:T(8,128)(2,1)} all-gather(bf16[2,16,512]{2,1,0:T(8,128)(2,1)S(1)} %get-tuple-element.1075), channel_id=1, replica_groups=mesh['seq'=8,'req'=32] {'seq'}, dimensions={0}, use_global_device_ids=true | all-gather | bytes 294912 | tf_op jit(solution)/shard_map/all_gather | solution.py:230
  92.3 15.7 %all_gather.121 = bf16[16,16,512]{2,1,0:T(8,128)(2,1)} all-gather(bf16[2,16,512]{2,1,0:T(8,128)(2,1)S(1)} %get-tuple-element.1074), channel_id=1, replica_groups=mesh['seq'=8,'req'=32] {'seq'}, dimensions={0}, use_global_device_ids=true | all-gather | bytes 294912 | tf_op jit(solution)/shard_map/all_gather | solution.py:231
  111.2 15.7 %all_gather.125 = bf16[16,16,512]{2,1,0:T(8,128)(2,1)} all-gather(bf16[2,16,512]{2,1,0:T(8,128)(2,1)S(1)} %get-tuple-element.1073), channel_id=1, replica_groups=mesh['seq'=8,'req'=32] {'seq'}, dimensions={0}, use_global_device_ids=true | all-gather | bytes 294912 | tf_op jit(solution)/shard_map/all_gather | solution.py:230
  127.6 15.7 %all_gather.129 = bf16[16,16,512]{2,1,0:T(8,128)(2,1)} all-gather(bf16[2,16,512]{2,1,0:T(8,128)(2,1)S(1)} %get-tuple-element.1072), channel_id=1, replica_groups=mesh['seq'=8,'req'=32] {'seq'}, dimensions={0}, use_global_device_ids=true | all-gather | bytes 294912 | tf_op jit(solution)/shard_map/all_gather | solution.py:231
  147.0 15.7 %all_gather.133 = bf16[16,16,512]{2,1,0:T(8,128)(2,1)} all-gather(bf16[2,16,512]{2,1,0:T(8,128)(2,1)S(1)} %get-tuple-element.1071), channel_id=1, replica_groups=mesh['seq'=8,'req'=32] {'seq'}, dimensions={0}, use_global_device_ids=true | all-gather | bytes 294912 | tf_op jit(solution)/shard_map/all_gather | solution.py:230
  167.3 20.3 %all_gather.109 = bf16[16,4,1536]{0,1,2:T(4,128)(2,1)S(1)} all-gather(bf16[16,4,192]{0,1,2:T(4,128)(2,1)S(1)} %bitcast.396), channel_id=1, replica_groups=mesh['seq'=8,'req'=32] {'seq'}, dimensions={2}, use_global_device_ids=true | all-gather | bytes 221184 | tf_op jit(solution)/shard_map/all_gather | solution.py:188
  209.1 16.2 %all_gather.137 = bf16[16,16,512]{2,1,0:T(8,128)(2,1)} all-gather(bf16[2,16,512]{2,1,0:T(8,128)(2,1)S(1)} %copy-done.31), channel_id=1, replica_groups=mesh['seq'=8,'req'=32] {'seq'}, dimensions={0}, use_global_device_ids=true | all-gather | bytes 294912 | tf_op jit(solution)/shard_map/all_gather | solution.py:231
  277.7 16.9 %all_gather.118 = bf16[16,4,512]{2,1,0:T(4,128)(2,1)S(1)} all-gather(bf16[2,4,512]{2,1,0:T(4,128)(2,1)S(1)} %scatter.26), channel_id=1, replica_groups=mesh['seq'=8,'req'=32] {'seq'}, dimensions={0}, use_global_device_ids=true | all-gather | bytes 73728 | tf_op jit(solution)/shard_map/all_gather | solution.py:232
  295.5 14.5 %all_gather.122 = bf16[16,4,512]{2,1,0:T(4,128)(2,1)S(1)} all-gather(bf16[2,4,512]{2,1,0:T(4,128)(2,1)S(1)} %scatter.29), channel_id=1, replica_groups=mesh['seq'=8,'req'=32] {'seq'}, dimensions={0}, use_global_device_ids=true | all-gather | bytes 73728 | tf_op jit(solution)/shard_map/all_gather | solution.py:233
  326.9 14.6 %all_gather.130 = bf16[16,4,512]{2,1,0:T(4,128)(2,1)S(1)} all-gather(bf16[2,4,512]{2,1,0:T(4,128)(2,1)S(1)} %scatter.31), channel_id=1, replica_groups=mesh['seq'=8,'req'=32] {'seq'}, dimensions={0}, use_global_device_ids=true | all-gather | bytes 73728 | tf_op jit(solution)/shard_map/all_gather | solution.py:233
  343.6 14.6 %all_gather.134 = bf16[16,4,512]{2,1,0:T(4,128)(2,1)S(1)} all-gather(bf16[2,4,512]{2,1,0:T(4,128)(2,1)S(1)} %scatter.34), channel_id=1, replica_groups=mesh['seq'=8,'req'=32] {'seq'}, dimensions={0}, use_global_device_ids=true | all-gather | bytes 73728 | tf_op jit(solution)/shard_map/all_gather | solution.py:232
  399.3 14.6 %all-gather.11 = bf16[128,8,3]{1,2,0:T(4,128)(2,1)S(1)} all-gather(bf16[16,8,3]{1,2,0:T(4,128)(2,1)S(1)} %copy.349), channel_id=13, replica_groups=mesh['seq'=8,'req'=32] {'seq'}, dimensions={0}, use_global_device_ids=true | all-gather | bytes 6912 | tf_op jit(solution)/shard_map/all_gather | solution.py:18
  418.5 14.6 %all-gather.12 = bf16[128,8,3]{1,2,0:T(4,128)(2,1)S(1)} all-gather(bf16[16,8,3]{1,2,0:T(4,128)(2,1)S(1)} %copy.350), channel_id=14, replica_groups=mesh['seq'=8,'req'=32] {'seq'}, dimensions={0}, use_global_device_ids=true | all-gather | bytes 6912 | tf_op jit(solution)/shard_map/all_gather | solution.py:18
  438.1 15.3 %all-gather.13 = bf16[128,8,3,64]{3,0,2,1:T(8,128)(2,1)S(1)} all-gather(bf16[16,8,3,64]{3,0,2,1:T(8,128)(2,1)S(1)} %fusion.87), channel_id=15, replica_groups=mesh['seq'=8,'req'=32] {'seq'}, dimensions={0}, use_global_device_ids=true | all-gather | bytes 442368 | tf_op jit(solution)/shard_map/all_gather | solution.py:18
  457.7 33.8 %while.87 = (s32[]{:T(128)}, f32[16,8,3]{0,1,2:T(8,128)S(1)}, f32[16,8,3]{0,1,2:T(8,128)S(1)}, f32[16,8,3,64]{3,2,1,0:T(4,128)S(1)}, bf16[8,16,8,3]{1,2,3,0:T(8,...) while((s32[]{:T(128)}, f32[16,8,3]{0,1,2:T(8,128)S(1)}, ...), condition=%wide.region_35.38_spmd, body=%wide.region_34.37_spmd.sunk | while | flops 101381 | bytes 364183 | solution.py:30
  494.9 14.6 %all-gather.8 = bf16[128,8,3]{1,2,0:T(4,128)(2,1)S(1)} all-gather(bf16[16,8,3]{1,2,0:T(4,128)(2,1)S(1)} %copy.330), channel_id=10, replica_groups=mesh['seq'=8,'req'=32] {'seq'}, dimensions={0}, use_global_device_ids=true | all-gather | bytes 6912 | tf_op jit(solution)/shard_map/all_gather | solution.py:18
  512.0 14.6 %all-gather.9 = bf16[128,8,3]{1,2,0:T(4,128)(2,1)S(1)} all-gather(bf16[16,8,3]{1,2,0:T(4,128)(2,1)S(1)} %copy.331), channel_id=11, replica_groups=mesh['seq'=8,'req'=32] {'seq'}, dimensions={0}, use_global_device_ids=true | all-gather | bytes 6912 | tf_op jit(solution)/shard_map/all_gather | solution.py:18
  529.8 15.5 %all-gather.10 = bf16[128,8,3,64]{3,0,2,1:T(8,128)(2,1)S(1)} all-gather(bf16[16,8,3,64]{3,0,2,1:T(8,128)(2,1)S(1)} %fusion.86), channel_id=12, replica_groups=mesh['seq'=8,'req'=32] {'seq'}, dimensions={0}, use_global_device_ids=true | all-gather | bytes 442368 | tf_op jit(solution)/shard_map/all_gather | solution.py:18
  549.6 33.8 %while.86 = (s32[]{:T(128)}, f32[16,8,3]{0,1,2:T(8,128)S(1)}, f32[16,8,3]{0,1,2:T(8,128)S(1)}, f32[16,8,3,64]{3,2,1,0:T(4,128)S(1)}, bf16[8,16,8,3]{1,2,3,0:T(8,...) while((s32[]{:T(128)}, f32[16,8,3]{0,1,2:T(8,128)S(1)}, ...), condition=%wide.region_26.29_spmd, body=%wide.region_25.28_spmd.sunk | while | flops 101381 | bytes 364183 | solution.py:30
  590.0 14.6 %all-gather.5 = bf16[128,8,3]{1,2,0:T(4,128)(2,1)S(1)} all-gather(bf16[16,8,3]{1,2,0:T(4,128)(2,1)S(1)} %copy.310), channel_id=7, replica_groups=mesh['seq'=8,'req'=32] {'seq'}, dimensions={0}, use_global_device_ids=true | all-gather | bytes 6912 | tf_op jit(solution)/shard_map/all_gather | solution.py:18
  607.1 14.6 %all-gather.6 = bf16[128,8,3]{1,2,0:T(4,128)(2,1)S(1)} all-gather(bf16[16,8,3]{1,2,0:T(4,128)(2,1)S(1)} %copy.311), channel_id=8, replica_groups=mesh['seq'=8,'req'=32] {'seq'}, dimensions={0}, use_global_device_ids=true | all-gather | bytes 6912 | tf_op jit(solution)/shard_map/all_gather | solution.py:18
  624.9 15.8 %all-gather.7 = bf16[128,8,3,64]{3,0,2,1:T(8,128)(2,1)S(1)} all-gather(bf16[16,8,3,64]{3,0,2,1:T(8,128)(2,1)S(1)} %fusion.85), channel_id=9, replica_groups=mesh['seq'=8,'req'=32] {'seq'}, dimensions={0}, use_global_device_ids=true | all-gather | bytes 442368 | tf_op jit(solution)/shard_map/all_gather | solution.py:18
  645.0 33.6 %while.85 = (s32[]{:T(128)}, f32[16,8,3]{0,1,2:T(8,128)S(1)}, f32[16,8,3]{0,1,2:T(8,128)S(1)}, f32[16,8,3,64]{3,2,1,0:T(4,128)S(1)}, bf16[8,16,8,3]{1,2,3,0:T(8,...) while((s32[]{:T(128)}, f32[16,8,3]{0,1,2:T(8,128)S(1)}, ...), condition=%wide.region_17.20_spmd, body=%wide.region_16.19_spmd.sunk | while | flops 101381 | bytes 364183 | solution.py:30
  683.3 14.6 %all-gather.1 = bf16[128,8,3]{1,2,0:T(4,128)(2,1)S(1)} all-gather(bf16[16,8,3]{1,2,0:T(4,128)(2,1)S(1)} %copy.285), channel_id=3, replica_groups=mesh['seq'=8,'req'=32] {'seq'}, dimensions={0}, use_global_device_ids=true | all-gather | bytes 6912 | tf_op jit(solution)/shard_map/all_gather | solution.py:18
  700.5 14.6 %all-gather.2 = bf16[128,8,3]{1,2,0:T(4,128)(2,1)S(1)} all-gather(bf16[16,8,3]{1,2,0:T(4,128)(2,1)S(1)} %copy.286), channel_id=4, replica_groups=mesh['seq'=8,'req'=32] {'seq'}, dimensions={0}, use_global_device_ids=true | all-gather | bytes 6912 | tf_op jit(solution)/shard_map/all_gather | solution.py:18
  718.2 15.5 %all-gather.4 = bf16[128,8,3,64]{3,0,2,1:T(8,128)(2,1)S(1)} all-gather(bf16[16,8,3,64]{3,0,2,1:T(8,128)(2,1)S(1)} %fusion.84), channel_id=6, replica_groups=mesh['seq'=8,'req'=32] {'seq'}, dimensions={0}, use_global_device_ids=true | all-gather | bytes 442368 | tf_op jit(solution)/shard_map/all_gather | solution.py:18
  738.0 33.7 %while.84 = (s32[]{:T(128)}, f32[16,8,3]{0,1,2:T(8,128)S(1)}, f32[16,8,3]{0,1,2:T(8,128)S(1)}, f32[16,8,3,64]{3,2,1,0:T(4,128)S(1)}, bf16[8,16,8,3]{1,2,3,0:T(8,...) while((s32[]{:T(128)}, f32[16,8,3]{0,1,2:T(8,128)S(1)}, ...), condition=%wide.region_8.11_spmd, body=%wide.region_7.10_spmd.sunk | while | flops 101381 | bytes 364183 | solution.py:30
  776.5 72.4 %all-reduce.7.cloned.1.call-done = (bf16[16,1536]{1,0:T(8,128)(2,1)}, bf16[16,1536]{1,0:T(8,128)(2,1)}, bf16[16,1536]{1,0:T(8,128)(2,1)}, bf16[16,1536]{1,0:T(8,128)(2,1)}) async-done(((bf16[16,1536]{1,0:T(8,128)(2,1)}, bf16[16,1536]{1,0:T(8,128)(2,1)}, bf16[16,1536]{1,0:T(8,128)(2,1)}, bf16[16,1536]{1,0:T(8,128)(2,1)}), (bf16[16,1536]{1,0:T(8,128)(2,1)}, bf16[16,1536]{1,0:T(8,128)(2,1)}, ...) | async-done | bytes 196624
  853.5 16.4 %all_to_all.46 = bf16[32,1,4,1536]{3,2,1,0:T(4,128)(2,1)S(1)} all-to-all(bf16[32,1,4,1536]{3,2,1,0:T(4,128)(2,1)} %bitcast.395), channel_id=1, replica_groups=mesh['seq'=8,'req'=32] {'req'}, dimensions={0} | all-to-all | bytes 786432 | tf_op jit(solution)/shard_map/all_to_all | solution.py:214
  (528 shorter events, 383.5 us)
Async XLA Ops:
  7.2 862.7 %copy-start = (bf16[1,1536,1024]{2,1,0:T(8,128)(2,1)S(1)}, bf16[1,1536,1024]{2,1,0:T(8,128)(2,1)}, u32[]{:S(2)}) copy-start(bf16[1,1536,1024]{2,1,0:T(8,128)(2,1)} %param.58) | copy-start | bytes 9437188
  7.2 156.3 %copy-start.26 = (bf16[1,2,4,1536]{3,2,1,0:T(4,128)(2,1)S(1)}, bf16[1,2,4,1536]{3,2,1,0:T(4,128)(2,1)}, u32[]{:S(2)}) copy-start(bf16[1,2,4,1536]{3,2,1,0:T(4,128)(2,1)} %param.45) | copy-start | bytes 73732
  29.6 242.2 %all-to-all-start = ((bf16[8,2,256]{2,1,0:T(2,128)(2,1)}), bf16[8,2,256]{2,1,0:T(2,128)(2,1)}, u32[]{:S(2)}, u32[]{:S(2)}) async-start(bf16[8,2,256]{2,1,0:T(2,128)(2,1)} %reshape.1151), calls=%async_computation | async-start | bytes 16384 | tf_op jit(solution)/shard_map/all_to_all | solution.py:190
  38.5 69.6 %copy-start.63 = (pred[2]{0:T(512)(128)(4,1)}, pred[2]{0:T(512)(128)(4,1)S(1)}, u32[]{:S(2)}) copy-start(pred[2]{0:T(512)(128)(4,1)S(1)} %get-tuple-element.1064) | copy-start | bytes 10
  38.5 149.1 %copy-start.61 = (pred[2]{0:T(512)(128)(4,1)}, pred[2]{0:T(512)(128)(4,1)S(1)}, u32[]{:S(2)}) copy-start(pred[2]{0:T(512)(128)(4,1)S(1)} %get-tuple-element.1060) | copy-start | bytes 10
  38.5 149.1 %copy-start.62 = (pred[2]{0:T(512)(128)(4,1)}, pred[2]{0:T(512)(128)(4,1)S(1)}, u32[]{:S(2)}) copy-start(pred[2]{0:T(512)(128)(4,1)S(1)} %get-tuple-element.1062) | copy-start | bytes 10
  38.5 69.5 %copy-start.59 = (s32[1024]{0:T(1024)}, s32[1024]{0:T(1024)S(1)}, u32[]{:S(2)}) copy-start(s32[1024]{0:T(1024)S(1)} %pad_clamp_fusion.3) | copy-start | bytes 12292
  75.9 89.8 %copy-start.27 = (bf16[2,16,512]{2,1,0:T(8,128)(2,1)}, bf16[2,16,512]{2,1,0:T(8,128)(2,1)S(1)}, u32[]{:S(2)}) copy-start(bf16[2,16,512]{2,1,0:T(8,128)(2,1)S(1)} %get-tuple-element.1074) | copy-start | bytes 98308
  92.3 18.7 %copy-start.57 = (s32[1024]{0:T(1024)}, s32[1024]{0:T(1024)S(1)}, u32[]{:S(2)}) copy-start(s32[1024]{0:T(1024)S(1)} %pad_clamp_fusion.2) | copy-start | bytes 12292
  111.2 54.5 %copy-start.29 = (bf16[2,16,512]{2,1,0:T(8,128)(2,1)}, bf16[2,16,512]{2,1,0:T(8,128)(2,1)S(1)}, u32[]{:S(2)}) copy-start(bf16[2,16,512]{2,1,0:T(8,128)(2,1)S(1)} %get-tuple-element.1072) | copy-start | bytes 98308
  127.6 18.7 %copy-start.56 = (s32[1024]{0:T(1024)}, s32[1024]{0:T(1024)S(1)}, u32[]{:S(2)}) copy-start(s32[1024]{0:T(1024)S(1)} %pad_clamp_fusion.1) | copy-start | bytes 12292
  191.2 17.9 %copy-start.31 = (bf16[2,16,512]{2,1,0:T(8,128)(2,1)S(1)}, bf16[2,16,512]{2,1,0:T(8,128)(2,1)}, u32[]{:S(2)}) copy-start(bf16[2,16,512]{2,1,0:T(8,128)(2,1)} %get-tuple-element.1070) | copy-start | bytes 98308
  193.5 34.8 %copy-start.60 = (pred[2]{0:T(512)(128)(4,1)S(1)}, pred[2]{0:T(512)(128)(4,1)}, u32[]{:S(2)}) copy-start(pred[2]{0:T(512)(128)(4,1)} %get-tuple-element.1032) | copy-start | bytes 10
  196.4 68.7 %copy-start.34 = (bf16[2,4,512]{2,1,0:T(4,128)(2,1)}, bf16[2,4,512]{2,1,0:T(4,128)(2,1)S(1)}, u32[]{:S(2)}) copy-start(bf16[2,4,512]{2,1,0:T(4,128)(2,1)S(1)} %broadcast_select_fusion.14) | copy-start | bytes 24580
  198.1 31.0 %copy-start.73 = (s32[2]{0:T(128)S(1)}, s32[2]{0:T(128)}, u32[]{:S(2)}) copy-start(s32[2]{0:T(128)} %iota_add_fusion) | copy-start | bytes 28
  198.8 29.5 %copy-start.58 = (s32[1024]{0:T(1024)}, s32[1024]{0:T(1024)S(1)}, u32[]{:S(2)}) copy-start(s32[1024]{0:T(1024)S(1)} %pad_clamp_fusion) | copy-start | bytes 12292
  228.4 41.4 %copy-start.32 = (bf16[2,16,512]{2,1,0:T(8,128)(2,1)}, bf16[2,16,512]{2,1,0:T(8,128)(2,1)S(1)}, u32[]{:S(2)}) copy-start(bf16[2,16,512]{2,1,0:T(8,128)(2,1)S(1)} %get-tuple-element.1068) | copy-start | bytes 98308
  229.3 30.6 %copy-start.37 = (pred[16,32]{1,0:T(8,128)(4,1)}, pred[16,32]{1,0:T(8,128)(4,1)S(1)}, u32[]{:S(2)}) copy-start(pred[16,32]{1,0:T(8,128)(4,1)S(1)} %iota_compare_fusion.6) | copy-start | bytes 1540
  262.4 117.7 %copy-start.51 = (pred[16,8]{0,1:T(8,128)(4,1)}, pred[16,8]{0,1:T(8,128)(4,1)S(1)}, u32[]{:S(2)}) copy-start(pred[16,8]{0,1:T(8,128)(4,1)S(1)} %get-tuple-element.1085) | copy-start | bytes 388
  265.1 30.3 %copy-start.35 = (bf16[2,4,512]{2,1,0:T(4,128)(2,1)S(1)}, bf16[2,4,512]{2,1,0:T(4,128)(2,1)}, u32[]{:S(2)}) copy-start(bf16[2,4,512]{2,1,0:T(4,128)(2,1)} %copy-done.34) | copy-start | bytes 24580
  265.1 112.8 %copy-start.52 = (pred[16,8]{0,1:T(8,128)(4,1)S(1)}, pred[16,8]{0,1:T(8,128)(4,1)}, u32[]{:S(2)}) copy-start(pred[16,8]{0,1:T(8,128)(4,1)} %get-tuple-element.1083) | copy-start | bytes 388
  265.9 118.1 %copy-start.43 = (f32[16,8,3]{0,2,1:T(4,128)S(1)}, f32[16,8,3]{0,2,1:T(4,128)}, u32[]{:S(2)}) copy-start(f32[16,8,3]{0,2,1:T(4,128)} %get-tuple-element.1088) | copy-start | bytes 4612
  265.9 119.4 %copy-start.45 = (f32[16,8,3]{0,2,1:T(4,128)S(1)}, f32[16,8,3]{0,2,1:T(4,128)}, u32[]{:S(2)}) copy-start(f32[16,8,3]{0,2,1:T(4,128)} %get-tuple-element.1106) | copy-start | bytes 4612
  271.8 22.9 %all-to-all-start.1 = ((bf16[8,2,256]{2,1,0:T(2,128)(2,1)}), bf16[8,2,256]{2,1,0:T(2,128)(2,1)S(1)}, u32[]{:S(2)}, u32[]{:S(2)}) async-start(bf16[8,2,256]{2,1,0:T(2,128)(2,1)} %reshape.1153), calls=%async_computation.1 | async-start | bytes 16384 | tf_op jit(solution)/shard_map/all_to_all | solution.py:191
  276.7 572.2 %all-reduce.7.cloned.1.call-start = ((), (), s32[]{:S(2)}) async-start(), calls=%async_computation.4 | async-start | bytes 393216
  386.6 28.8 %copy-start.25 = (f32[16,8,3]{0,2,1:T(4,128)}, f32[16,8,3]{0,2,1:T(4,128)S(1)}, u32[]{:S(2)}) copy-start(f32[16,8,3]{0,2,1:T(4,128)S(1)} %get-tuple-element.1029) | copy-start | bytes 4612
  392.7 22.7 %copy-start.24 = (f32[16,8,3]{0,2,1:T(4,128)}, f32[16,8,3]{0,2,1:T(4,128)S(1)}, u32[]{:S(2)}) copy-start(f32[16,8,3]{0,2,1:T(4,128)S(1)} %get-tuple-element.1027) | copy-start | bytes 4612
  394.8 20.6 %copy-start.23 = (f32[16,8,3]{0,2,1:T(4,128)}, f32[16,8,3]{0,2,1:T(4,128)S(1)}, u32[]{:S(2)}) copy-start(f32[16,8,3]{0,2,1:T(4,128)S(1)} %get-tuple-element.1025) | copy-start | bytes 4612
  397.8 17.6 %copy-start.14 = (f32[16,8,3,32]{3,0,2,1:T(8,128)S(1)}, f32[16,8,3,32]{3,0,2,1:T(8,128)}, u32[]{:S(2)}) copy-start(f32[16,8,3,32]{3,0,2,1:T(8,128)} %get-tuple-element.1097) | copy-start | bytes 147460
  397.8 17.6 %copy-start.38 = (pred[16,32]{1,0:T(8,128)(4,1)S(1)}, pred[16,32]{1,0:T(8,128)(4,1)}, u32[]{:S(2)}) copy-start(pred[16,32]{1,0:T(8,128)(4,1)} %copy-done.37) | copy-start | bytes 1540
  853.5 17.0 %copy-start.71 = (bf16[1,512,1536]{2,1,0:T(8,128)(2,1)S(1)}, bf16[1,512,1536]{2,1,0:T(8,128)(2,1)}, u32[]{:S(2)}) copy-start(bf16[1,512,1536]{2,1,0:T(8,128)(2,1)} %param.59) | copy-start | bytes 4718596
  871.9 13.6 %all-to-all-start.3 = ((bf16[32,1,4,1536]{3,2,1,0:T(4,128)(2,1)}), bf16[32,1,4,1536]{3,2,1,0:T(4,128)(2,1)S(1)}, u32[]{:S(2)}, u32[]{:S(2)}) async-start(bf16[32,1,4,1536]{3,2,1,0:T(4,128)(2,1)} %copy.366), calls=%async_computation.3 | async-start | bytes 786432 | tf_op jit(solution)/shard_map/all_to_all | solution.py:212
  (46 other events, 224.2 us)
Sparse Core Ops, SparseCore 0:
  775.7 73.1 all-reduce.6
where the time goes:
time: 908 us; the launch traced here: 895 us
  blocking collectives  452 us (50%)
  local copies, waits for them, and re-layouts  168 us (19%)
  other arithmetic  103 us (11%)
  waiting for transfers between devices  76.4 us (8%)
  matrix products  64.6 us (7%)
  between operations  15.8 us (2%)
  starting transfers between devices  14.6 us (2%)
    all_gather x12, blocking collectives, merged(): lax.all_gather(a.astype(kind), axis)  179 us
    unnamed x2, waiting for transfers between devices  72.4 us
    all_gather x4, blocking collectives, local(): lax.all_gather(beam_value_cache, 'seq', axis=0, tiled=True)  65.9 us
    all_gather x4, blocking collectives, local(): lax.all_gather(beam_key_cache, 'seq', axis=0, tiled=True)  63.1 us
    add x28, other arithmetic, join_partials(): first_scale[..., None] * first_part[2]  46.6 us
    all_gather x3, blocking collectives, local(): lax.all_gather(newest_key, 'seq', axis=0, tiled=True)  46 us
    all_gather x3, blocking collectives, local(): lax.all_gather(newest_value, 'seq', axis=0, tiled=True)  43.7 us
    dot_general x12, matrix products, local_partial(): jnp.einsum('bgjd,kgd->bgjk', decode_query_step, shaped_keys, preferred_el...  29.1 us
  transfers between devices with their start and end apart: 4, of which 2 were waited for; matrix products, arithmetic and copies ran while one was open for 10% of the time, Pallas kernels for 0%

commit v1 on v0

--- a/solution.py
+++ b/solution.py
@@ -226,11 +226,17 @@
     hidden_rows = []
     for decode_step_index in range(step_count):
         chosen_rows = my_parents[decode_step_index]
+
+        def part_inputs(field_in):
+            return jnp.concatenate(
+                jax.lax.all_to_all(jnp.stack([field_in] * jax.lax.axis_size("seq")), "seq", 0, 0), 0
+            )
+
         received = (
             lax.all_gather(beam_key_cache, "seq", axis=0, tiled=True),
             lax.all_gather(beam_value_cache, "seq", axis=0, tiled=True),
             lax.all_gather(newest_key, "seq", axis=0, tiled=True),
-            lax.all_gather(newest_value, "seq", axis=0, tiled=True),
+            part_inputs(newest_value),
         )
         beam_key_cache = jnp.take(received[0], chosen_rows, axis=0)
         beam_value_cache = jnp.take(received[1], chosen_rows, axis=0)

time: 908 us -> 930 us (1.024)
  blocking collectives: 452 us -> 416 us
  other arithmetic: 103 us -> 128 us
  local copies, waits for them, and re-layouts: 168 us -> 189 us
  starting transfers between devices: 14.6 us -> 29 us
    all_gather x3 -> x0, blocking collectives: 43.7 us -> none  [local(): lax.all_gather(newest_value, 'seq', axis=0, tiled=True)]
    all_to_all x0 -> x3, starting transfers between devices: none -> 14.4 us  [part_inputs(): jax.lax.all_to_all(jnp.stack([field_in] * jax.lax.axis_size('seq')), 'seq...]
    unnamed x158 -> x154, local copies, waits for them, and re-layouts: 21.2 us -> 21.8 us
  transfers between devices with their start and end apart: 4 -> 7, of which waited for: 2 -> 2; matrix products, arithmetic and copies ran while one was open for 10% -> 15% of each run, Pallas kernels for 0% -> 0%
where the time goes in v1:
time: 930 us; the launch traced here: 917 us
  blocking collectives  416 us (45%)
  local copies, waits for them, and re-layouts  189 us (20%)
  other arithmetic  128 us (14%)
  waiting for transfers between devices  76.6 us (8%)
  matrix products  62.6 us (7%)
  starting transfers between devices  29 us (3%)
  between operations  15.8 us (2%)
    all_gather x12, blocking collectives, merged(): lax.all_gather(a.astype(kind), axis)  186 us
    unnamed x2, waiting for transfers between devices  72.7 us
    all_gather x4, blocking collectives, local(): lax.all_gather(beam_value_cache, 'seq', axis=0, tiled=True)  65.9 us
    all_gather x4, blocking collectives, local(): lax.all_gather(beam_key_cache, 'seq', axis=0, tiled=True)  63.1 us
    add x28, other arithmetic, join_partials(): first_scale[..., None] * first_part[2]  54.4 us
    all_gather x3, blocking collectives, local(): lax.all_gather(newest_key, 'seq', axis=0, tiled=True)  46.1 us
    add x28, other arithmetic, join_partials(): denominator = first_scale * first_part[1] + second_scale * second_part[1]  28.7 us
    dot_general x12, matrix products, local_partial(): jnp.einsum('bgjd,kgd->bgjk', decode_query_step, shaped_keys, preferred_el...  28.4 us
  transfers between devices with their start and end apart: 7, of which 2 were waited for; matrix products, arithmetic and copies ran while one was open for 15% of the time, Pallas kernels for 0%

profile of v1, /device:TPU:8, one launch (start us, length us, event | category | flops | bytes accessed | tf_op | source)
XLA Modules:
  0.0 916.7 jit_solution(4067783848821951426)
XLA Ops:
  9.3 18.2 %all_gather.96 = bf16[16,4,1536]{2,1,0:T(4,128)(2,1)S(1)} all-gather(bf16[2,4,1536]{2,1,0:T(4,128)(2,1)S(1)} %fusion.149), channel_id=1, replica_groups=mesh['seq'=8,'req'=32] {'seq'}, dimensions={0}, use_global_device_ids=true | all-gather | bytes 221184 | tf_op jit(solution)/shard_map/all_gather | solution.py:180
  38.4 18.3 %all-gather.3 = bf16[1,16,16,512]{3,2,0,1:T(8,128)(2,1)} all-gather(bf16[1,2,16,512]{3,2,0,1:T(8,128)(2,1)} %bitcast.432), channel_id=5, replica_groups=mesh['seq'=8,'req'=32] {'seq'}, dimensions={1}, use_global_device_ids=true | all-gather | bytes 294912 | tf_op jit(solution)/shard_map/all_gather | solution.py:237
  56.7 16.0 %all-gather = bf16[1,16,16,512]{3,2,0,1:T(8,128)(2,1)} all-gather(bf16[1,2,16,512]{3,2,0,1:T(8,128)(2,1)} %bitcast.433), channel_id=2, replica_groups=mesh['seq'=8,'req'=32] {'seq'}, dimensions={1}, use_global_device_ids=true | all-gather | bytes 294912 | tf_op jit(solution)/shard_map/all_gather | solution.py:236
  75.8 15.7 %all_gather.104 = bf16[16,16,512]{2,1,0:T(8,128)(2,1)} all-gather(bf16[2,16,512]{2,1,0:T(8,128)(2,1)S(1)} %get-tuple-element.1075), channel_id=1, replica_groups=mesh['seq'=8,'req'=32] {'seq'}, dimensions={0}, use_global_device_ids=true | all-gather | bytes 294912 | tf_op jit(solution)/shard_map/all_gather | solution.py:236
  92.2 15.7 %all_gather.108 = bf16[16,16,512]{2,1,0:T(8,128)(2,1)} all-gather(bf16[2,16,512]{2,1,0:T(8,128)(2,1)S(1)} %get-tuple-element.1074), channel_id=1, replica_groups=mesh['seq'=8,'req'=32] {'seq'}, dimensions={0}, use_global_device_ids=true | all-gather | bytes 294912 | tf_op jit(solution)/shard_map/all_gather | solution.py:237
  111.1 15.7 %all_gather.111 = bf16[16,16,512]{2,1,0:T(8,128)(2,1)} all-gather(bf16[2,16,512]{2,1,0:T(8,128)(2,1)S(1)} %get-tuple-element.1073), channel_id=1, replica_groups=mesh['seq'=8,'req'=32] {'seq'}, dimensions={0}, use_global_device_ids=true | all-gather | bytes 294912 | tf_op jit(solution)/shard_map/all_gather | solution.py:236
  127.5 15.7 %all_gather.115 = bf16[16,16,512]{2,1,0:T(8,128)(2,1)} all-gather(bf16[2,16,512]{2,1,0:T(8,128)(2,1)S(1)} %get-tuple-element.1072), channel_id=1, replica_groups=mesh['seq'=8,'req'=32] {'seq'}, dimensions={0}, use_global_device_ids=true | all-gather | bytes 294912 | tf_op jit(solution)/shard_map/all_gather | solution.py:237
  146.9 15.7 %all_gather.118 = bf16[16,16,512]{2,1,0:T(8,128)(2,1)} all-gather(bf16[2,16,512]{2,1,0:T(8,128)(2,1)S(1)} %get-tuple-element.1071), channel_id=1, replica_groups=mesh['seq'=8,'req'=32] {'seq'}, dimensions={0}, use_global_device_ids=true | all-gather | bytes 294912 | tf_op jit(solution)/shard_map/all_gather | solution.py:236
  167.3 20.3 %all_gather.97 = bf16[16,4,1536]{0,1,2:T(4,128)(2,1)S(1)} all-gather(bf16[16,4,192]{0,1,2:T(4,128)(2,1)S(1)} %bitcast.399), channel_id=1, replica_groups=mesh['seq'=8,'req'=32] {'seq'}, dimensions={2}, use_global_device_ids=true | all-gather | bytes 221184 | tf_op jit(solution)/shard_map/all_gather | solution.py:188
  209.1 16.2 %all_gather.122 = bf16[16,16,512]{2,1,0:T(8,128)(2,1)} all-gather(bf16[2,16,512]{2,1,0:T(8,128)(2,1)S(1)} %copy-done.32), channel_id=1, replica_groups=mesh['seq'=8,'req'=32] {'seq'}, dimensions={0}, use_global_device_ids=true | all-gather | bytes 294912 | tf_op jit(solution)/shard_map/all_gather | solution.py:237
  279.0 16.9 %all_gather.105 = bf16[16,4,512]{2,1,0:T(4,128)(2,1)S(1)} all-gather(bf16[2,4,512]{2,1,0:T(4,128)(2,1)S(1)} %scatter.26), channel_id=1, replica_groups=mesh['seq'=8,'req'=32] {'seq'}, dimensions={0}, use_global_device_ids=true | all-gather | bytes 73728 | tf_op jit(solution)/shard_map/all_gather | solution.py:238
  306.1 16.9 %all-gather.1 = bf16[128,8,3]{1,2,0:T(4,128)(2,1)S(1)} all-gather(bf16[16,8,3]{1,2,0:T(4,128)(2,1)S(1)} %copy.294), channel_id=3, replica_groups=mesh['seq'=8,'req'=32] {'seq'}, dimensions={0}, use_global_device_ids=true | all-gather | bytes 6912 | tf_op jit(solution)/shard_map/all_gather | solution.py:18
  329.0 15.6 %all-gather.4 = bf16[128,8,3,64]{3,0,2,1:T(8,128)(2,1)S(1)} all-gather(bf16[16,8,3,64]{3,0,2,1:T(8,128)(2,1)S(1)} %fusion.84), channel_id=6, replica_groups=mesh['seq'=8,'req'=32] {'seq'}, dimensions={0}, use_global_device_ids=true | all-gather | bytes 442368 | tf_op jit(solution)/shard_map/all_gather | solution.py:18
  350.8 14.5 %all_gather.112 = bf16[16,4,512]{2,1,0:T(4,128)(2,1)S(1)} all-gather(bf16[2,4,512]{2,1,0:T(4,128)(2,1)S(1)} %scatter.30), channel_id=1, replica_groups=mesh['seq'=8,'req'=32] {'seq'}, dimensions={0}, use_global_device_ids=true | all-gather | bytes 73728 | tf_op jit(solution)/shard_map/all_gather | solution.py:238
  376.7 17.1 %all-gather.5 = bf16[128,8,3]{1,2,0:T(4,128)(2,1)S(1)} all-gather(bf16[16,8,3]{1,2,0:T(4,128)(2,1)} %copy.319), channel_id=7, replica_groups=mesh['seq'=8,'req'=32] {'seq'}, dimensions={0}, use_global_device_ids=true | all-gather | bytes 6912 | tf_op jit(solution)/shard_map/all_gather | solution.py:18
  401.1 15.5 %all-gather.7 = bf16[128,8,3,64]{3,0,2,1:T(8,128)(2,1)S(1)} all-gather(bf16[16,8,3,64]{3,0,2,1:T(8,128)(2,1)S(1)} %fusion.85), channel_id=9, replica_groups=mesh['seq'=8,'req'=32] {'seq'}, dimensions={0}, use_global_device_ids=true | all-gather | bytes 442368 | tf_op jit(solution)/shard_map/all_gather | solution.py:18
  424.2 14.6 %all_gather.119 = bf16[16,4,512]{2,1,0:T(4,128)(2,1)S(1)} all-gather(bf16[2,4,512]{2,1,0:T(4,128)(2,1)S(1)} %scatter.34), channel_id=1, replica_groups=mesh['seq'=8,'req'=32] {'seq'}, dimensions={0}, use_global_device_ids=true | all-gather | bytes 73728 | tf_op jit(solution)/shard_map/all_gather | solution.py:238
  451.1 17.1 %all-gather.8 = bf16[128,8,3]{1,2,0:T(4,128)(2,1)S(1)} all-gather(bf16[16,8,3]{1,2,0:T(4,128)(2,1)} %copy.339), channel_id=10, replica_groups=mesh['seq'=8,'req'=32] {'seq'}, dimensions={0}, use_global_device_ids=true | all-gather | bytes 6912 | tf_op jit(solution)/shard_map/all_gather | solution.py:18
  474.8 15.3 %all-gather.10 = bf16[128,8,3,64]{3,0,2,1:T(8,128)(2,1)S(1)} all-gather(bf16[16,8,3,64]{3,0,2,1:T(8,128)(2,1)S(1)} %fusion.86), channel_id=12, replica_groups=mesh['seq'=8,'req'=32] {'seq'}, dimensions={0}, use_global_device_ids=true | all-gather | bytes 442368 | tf_op jit(solution)/shard_map/all_gather | solution.py:18
  501.7 7.3 fusion.23
  511.8 14.8 %all-gather.11 = bf16[128,8,3]{1,2,0:T(4,128)(2,1)S(1)} all-gather(bf16[16,8,3]{1,2,0:T(4,128)(2,1)} %copy.358), channel_id=13, replica_groups=mesh['seq'=8,'req'=32] {'seq'}, dimensions={0}, use_global_device_ids=true | all-gather | bytes 6912 | tf_op jit(solution)/shard_map/all_gather | solution.py:18
  533.4 14.6 %all-gather.12 = bf16[128,8,3]{1,2,0:T(4,128)(2,1)S(1)} all-gather(bf16[16,8,3]{1,2,0:T(4,128)(2,1)S(1)} %copy.359), channel_id=14, replica_groups=mesh['seq'=8,'req'=32] {'seq'}, dimensions={0}, use_global_device_ids=true | all-gather | bytes 6912 | tf_op jit(solution)/shard_map/all_gather | solution.py:18
  554.4 15.4 %all-gather.13 = bf16[128,8,3,64]{3,0,2,1:T(8,128)(2,1)S(1)} all-gather(bf16[16,8,3,64]{3,0,2,1:T(8,128)(2,1)S(1)} %fusion.87), channel_id=15, replica_groups=mesh['seq'=8,'req'=32] {'seq'}, dimensions={0}, use_global_device_ids=true | all-gather | bytes 442368 | tf_op jit(solution)/shard_map/all_gather | solution.py:18
  574.8 40.3 %while.87 = (s32[]{:T(128)}, f32[16,8,3]{0,1,2:T(8,128)}, f32[16,8,3]{0,1,2:T(8,128)S(1)}, f32[16,8,3,64]{3,2,1,0:T(4,128)}, bf16[8,16,8,3]{1,2,3,0:T(8,128)(2,1...) while((s32[]{:T(128)}, f32[16,8,3]{0,1,2:T(8,128)}, ...), condition=%wide.region_35.38_spmd, body=%wide.region_34.37_spmd.sunk | while | flops 101381 | bytes 364183 | solution.py:30
  618.6 14.8 %all-gather.9 = bf16[128,8,3]{1,2,0:T(4,128)(2,1)S(1)} all-gather(bf16[16,8,3]{1,2,0:T(4,128)(2,1)S(1)} %copy.340), channel_id=11, replica_groups=mesh['seq'=8,'req'=32] {'seq'}, dimensions={0}, use_global_device_ids=true | all-gather | bytes 6912 | tf_op jit(solution)/shard_map/all_gather | solution.py:18
  635.8 36.3 %while.86 = (s32[]{:T(128)}, f32[16,8,3]{0,1,2:T(8,128)S(1)}, f32[16,8,3]{0,1,2:T(8,128)S(1)}, f32[16,8,3,64]{3,2,1,0:T(4,128)}, bf16[8,16,8,3]{1,2,3,0:T(8,128)...) while((s32[]{:T(128)}, f32[16,8,3]{0,1,2:T(8,128)S(1)}, ...), condition=%wide.region_26.29_spmd, body=%wide.region_25.28_spmd.sunk | while | flops 101381 | bytes 364183 | solution.py:30
  679.5 14.6 %all-gather.6 = bf16[128,8,3]{1,2,0:T(4,128)(2,1)S(1)} all-gather(bf16[16,8,3]{1,2,0:T(4,128)(2,1)S(1)} %copy.320), channel_id=8, replica_groups=mesh['seq'=8,'req'=32] {'seq'}, dimensions={0}, use_global_device_ids=true | all-gather | bytes 6912 | tf_op jit(solution)/shard_map/all_gather | solution.py:18
  696.4 40.1 %while.85 = (s32[]{:T(128)}, f32[16,8,3]{0,1,2:T(8,128)}, f32[16,8,3]{0,1,2:T(8,128)S(1)}, f32[16,8,3,64]{3,2,1,0:T(4,128)}, bf16[8,16,8,3]{1,2,3,0:T(8,128)(2,1...) while((s32[]{:T(128)}, f32[16,8,3]{0,1,2:T(8,128)}, ...), condition=%wide.region_17.20_spmd, body=%wide.region_16.19_spmd.sunk | while | flops 101381 | bytes 364183 | solution.py:30
  742.1 14.6 %all-gather.2 = bf16[128,8,3]{1,2,0:T(4,128)(2,1)S(1)} all-gather(bf16[16,8,3]{1,2,0:T(4,128)(2,1)S(1)} %copy.295), channel_id=4, replica_groups=mesh['seq'=8,'req'=32] {'seq'}, dimensions={0}, use_global_device_ids=true | all-gather | bytes 6912 | tf_op jit(solution)/shard_map/all_gather | solution.py:18
  759.0 33.8 %while.84 = (s32[]{:T(128)}, f32[16,8,3]{0,1,2:T(8,128)S(1)}, f32[16,8,3]{0,1,2:T(8,128)S(1)}, f32[16,8,3,64]{3,2,1,0:T(4,128)S(1)}, bf16[8,16,8,3]{1,2,3,0:T(8,...) while((s32[]{:T(128)}, f32[16,8,3]{0,1,2:T(8,128)S(1)}, ...), condition=%wide.region_8.11_spmd, body=%wide.region_7.10_spmd.sunk | while | flops 101381 | bytes 364183 | solution.py:30
  797.7 72.7 %all-reduce.7.cloned.1.call-done = (bf16[16,1536]{1,0:T(8,128)(2,1)}, bf16[16,1536]{1,0:T(8,128)(2,1)}, bf16[16,1536]{1,0:T(8,128)(2,1)}, bf16[16,1536]{1,0:T(8,128)(2,1)}) async-done(((bf16[16,1536]{1,0:T(8,128)(2,1)}, bf16[16,1536]{1,0:T(8,128)(2,1)}, bf16[16,1536]{1,0:T(8,128)(2,1)}, bf16[16,1536]{1,0:T(8,128)(2,1)}), (bf16[16,1536]{1,0:T(8,128)(2,1)}, bf16[16,1536]{1,0:T(8,128)(2,1)}, ...) | async-done | bytes 196624
  874.9 16.4 %all_to_all.62 = bf16[32,1,4,1536]{3,2,1,0:T(4,128)(2,1)S(1)} all-to-all(bf16[32,1,4,1536]{3,2,1,0:T(4,128)(2,1)} %bitcast.398), channel_id=1, replica_groups=mesh['seq'=8,'req'=32] {'req'}, dimensions={0} | all-to-all | bytes 786432 | tf_op jit(solution)/shard_map/all_to_all | solution.py:214
  (530 shorter events, 404.6 us)
Async XLA Ops:
  7.2 884.1 %copy-start = (bf16[1,1536,1024]{2,1,0:T(8,128)(2,1)S(1)}, bf16[1,1536,1024]{2,1,0:T(8,128)(2,1)}, u32[]{:S(2)}) copy-start(bf16[1,1536,1024]{2,1,0:T(8,128)(2,1)} %param.58) | copy-start | bytes 9437188
  7.2 156.2 %copy-start.27 = (bf16[1,2,4,1536]{3,2,1,0:T(4,128)(2,1)S(1)}, bf16[1,2,4,1536]{3,2,1,0:T(4,128)(2,1)}, u32[]{:S(2)}) copy-start(bf16[1,2,4,1536]{3,2,1,0:T(4,128)(2,1)} %param.45) | copy-start | bytes 73732
  29.6 243.0 %all-to-all-start = ((bf16[8,2,256]{2,1,0:T(2,128)(2,1)}), bf16[8,2,256]{2,1,0:T(2,128)(2,1)}, u32[]{:S(2)}, u32[]{:S(2)}) async-start(bf16[8,2,256]{2,1,0:T(2,128)(2,1)} %reshape.1170), calls=%async_computation | async-start | bytes 16384 | tf_op jit(solution)/shard_map/all_to_all | solution.py:190
  38.4 69.5 %copy-start.67 = (pred[2]{0:T(512)(128)(4,1)}, pred[2]{0:T(512)(128)(4,1)S(1)}, u32[]{:S(2)}) copy-start(pred[2]{0:T(512)(128)(4,1)S(1)} %get-tuple-element.1064) | copy-start | bytes 10
  38.4 149.1 %copy-start.65 = (pred[2]{0:T(512)(128)(4,1)}, pred[2]{0:T(512)(128)(4,1)S(1)}, u32[]{:S(2)}) copy-start(pred[2]{0:T(512)(128)(4,1)S(1)} %get-tuple-element.1060) | copy-start | bytes 10
  38.4 149.1 %copy-start.66 = (pred[2]{0:T(512)(128)(4,1)}, pred[2]{0:T(512)(128)(4,1)S(1)}, u32[]{:S(2)}) copy-start(pred[2]{0:T(512)(128)(4,1)S(1)} %get-tuple-element.1062) | copy-start | bytes 10
  38.4 69.5 %copy-start.63 = (s32[1024]{0:T(1024)}, s32[1024]{0:T(1024)S(1)}, u32[]{:S(2)}) copy-start(s32[1024]{0:T(1024)S(1)} %pad_clamp_fusion.3) | copy-start | bytes 12292
  75.8 89.8 %copy-start.28 = (bf16[2,16,512]{2,1,0:T(8,128)(2,1)}, bf16[2,16,512]{2,1,0:T(8,128)(2,1)S(1)}, u32[]{:S(2)}) copy-start(bf16[2,16,512]{2,1,0:T(8,128)(2,1)S(1)} %get-tuple-element.1074) | copy-start | bytes 98308
  111.1 54.5 %copy-start.30 = (bf16[2,16,512]{2,1,0:T(8,128)(2,1)}, bf16[2,16,512]{2,1,0:T(8,128)(2,1)S(1)}, u32[]{:S(2)}) copy-start(bf16[2,16,512]{2,1,0:T(8,128)(2,1)S(1)} %get-tuple-element.1072) | copy-start | bytes 98308
  193.4 45.9 %copy-start.8 = (bf16[16,8,3,64]{3,2,1,0:T(4,128)(2,1)}, bf16[16,8,3,64]{3,2,1,0:T(4,128)(2,1)S(1)}, u32[]{:S(2)}) copy-start(bf16[16,8,3,64]{3,2,1,0:T(4,128)(2,1)S(1)} %reshape_squeeze.29) | copy-start | bytes 147460
  193.4 34.9 %copy-start.64 = (pred[2]{0:T(512)(128)(4,1)S(1)}, pred[2]{0:T(512)(128)(4,1)}, u32[]{:S(2)}) copy-start(pred[2]{0:T(512)(128)(4,1)} %get-tuple-element.1032) | copy-start | bytes 10
  193.4 35.7 %copy-start.71 = (s32[2]{0:T(128)S(1)}, s32[2]{0:T(128)}, u32[]{:S(2)}) copy-start(s32[2]{0:T(128)} %iota_add_fusion) | copy-start | bytes 28
  196.4 68.2 %copy-start.38 = (bf16[2,4,512]{2,1,0:T(4,128)(2,1)}, bf16[2,4,512]{2,1,0:T(4,128)(2,1)S(1)}, u32[]{:S(2)}) copy-start(bf16[2,4,512]{2,1,0:T(4,128)(2,1)S(1)} %broadcast_select_fusion.14) | copy-start | bytes 24580
  198.8 37.5 %copy-start.60 = (s32[1024]{0:T(1024)}, s32[1024]{0:T(1024)S(1)}, u32[]{:S(2)}) copy-start(s32[1024]{0:T(1024)S(1)} %pad_clamp_fusion) | copy-start | bytes 12292
  209.1 43.9 %copy-start.41 = (pred[2048]{0:T(1024)(128)(4,1)}, pred[2048]{0:T(1024)(128)(4,1)S(1)}, u32[]{:S(2)}) copy-start(pred[2048]{0:T(1024)(128)(4,1)S(1)} %fusion.201) | copy-start | bytes 6148
  228.4 41.5 %copy-start.33 = (bf16[2,16,512]{2,1,0:T(8,128)(2,1)}, bf16[2,16,512]{2,1,0:T(8,128)(2,1)S(1)}, u32[]{:S(2)}) copy-start(bf16[2,16,512]{2,1,0:T(8,128)(2,1)S(1)} %get-tuple-element.1068) | copy-start | bytes 98308
  229.3 28.5 %copy-start.44 = (pred[16,32]{1,0:T(8,128)(4,1)}, pred[16,32]{1,0:T(8,128)(4,1)S(1)}, u32[]{:S(2)}) copy-start(pred[16,32]{1,0:T(8,128)(4,1)S(1)} %iota_compare_fusion.6) | copy-start | bytes 1540
  257.8 46.6 %copy-start.12 = (bf16[16,8,3,64]{3,2,1,0:T(4,128)(2,1)S(1)}, bf16[16,8,3,64]{3,2,1,0:T(4,128)(2,1)}, u32[]{:S(2)}) copy-start(bf16[16,8,3,64]{3,2,1,0:T(4,128)(2,1)} %copy-done.11) | copy-start | bytes 147460
  264.5 32.3 %copy-start.39 = (bf16[2,4,512]{2,1,0:T(4,128)(2,1)S(1)}, bf16[2,4,512]{2,1,0:T(4,128)(2,1)}, u32[]{:S(2)}) copy-start(bf16[2,4,512]{2,1,0:T(4,128)(2,1)} %copy-done.38) | copy-start | bytes 24580
  264.5 40.8 %copy-start.50 = (f32[16,8,3]{0,2,1:T(4,128)S(1)}, f32[16,8,3]{0,2,1:T(4,128)}, u32[]{:S(2)}) copy-start(f32[16,8,3]{0,2,1:T(4,128)} %get-tuple-element.1094) | copy-start | bytes 4612
  272.6 23.5 %all-to-all-start.1 = ((bf16[8,2,256]{2,1,0:T(2,128)(2,1)}), bf16[8,2,256]{2,1,0:T(2,128)(2,1)S(1)}, u32[]{:S(2)}, u32[]{:S(2)}) async-start(bf16[8,2,256]{2,1,0:T(2,128)(2,1)} %reshape.1172), calls=%async_computation.1 | async-start | bytes 16384 | tf_op jit(solution)/shard_map/all_to_all | solution.py:191
  298.2 49.6 %all-to-all-start.2 = ((bf16[8,2,4,512]{3,2,1,0:T(4,128)(2,1)}), bf16[8,2,4,512]{3,2,1,0:T(4,128)(2,1)}, u32[]{:S(2)}, u32[]{:S(2)}) async-start(bf16[8,2,4,512]{3,2,1,0:T(4,128)(2,1)} %stack.17), calls=%async_computation.2 | async-start | bytes 131072 | tf_op jit(solution)/shard_map/all_to_all | solution.py:232
  325.4 21.8 %copy-start.59 = (pred[16,8]{0,1:T(8,128)(4,1)S(1)}, pred[16,8]{0,1:T(8,128)(4,1)}, u32[]{:S(2)}) copy-start(pred[16,8]{0,1:T(8,128)(4,1)} %get-tuple-element.1085) | copy-start | bytes 388
  325.4 24.0 %copy-start.56 = (bf16[2,4,512]{2,1,0:T(4,128)(2,1)S(1)}, bf16[2,4,512]{2,1,0:T(4,128)(2,1)}, u32[]{:S(2)}) copy-start(bf16[2,4,512]{2,1,0:T(4,128)(2,1)} %gather_fusion.4) | copy-start | bytes 24580
  328.7 67.9 %copy-start.42 = (pred[2048]{0:T(1024)(128)(4,1)S(1)}, pred[2048]{0:T(1024)(128)(4,1)}, u32[]{:S(2)}) copy-start(pred[2048]{0:T(1024)(128)(4,1)} %copy-done.41) | copy-start | bytes 6148
  368.1 53.1 %all-to-all-start.3 = ((bf16[8,2,4,512]{3,2,1,0:T(4,128)(2,1)}), bf16[8,2,4,512]{3,2,1,0:T(4,128)(2,1)}, u32[]{:S(2)}, u32[]{:S(2)}) async-start(bf16[8,2,4,512]{3,2,1,0:T(4,128)(2,1)} %stack.19), calls=%async_computation.3 | async-start | bytes 131072 | tf_op jit(solution)/shard_map/all_to_all | solution.py:232
  396.5 26.2 %copy-start.57 = (bf16[2,4,512]{2,1,0:T(4,128)(2,1)S(1)}, bf16[2,4,512]{2,1,0:T(4,128)(2,1)}, u32[]{:S(2)}) copy-start(bf16[2,4,512]{2,1,0:T(4,128)(2,1)} %gather_fusion.8) | copy-start | bytes 24580
  441.0 53.8 %all-to-all-start.4 = ((bf16[8,2,4,512]{3,2,1,0:T(4,128)(2,1)}), bf16[8,2,4,512]{3,2,1,0:T(4,128)(2,1)}, u32[]{:S(2)}, u32[]{:S(2)}) async-start(bf16[8,2,4,512]{3,2,1,0:T(4,128)(2,1)} %stack.21), calls=%async_computation.4 | async-start | bytes 131072 | tf_op jit(solution)/shard_map/all_to_all | solution.py:232
  445.8 424.5 %all-reduce.7.cloned.1.call-start = ((), (), s32[]{:S(2)}) async-start(), calls=%async_computation.7 | async-start | bytes 393216
  574.8 61.0 %copy-start.26 = (f32[16,8,3]{0,1,2:T(8,128)S(1)}, f32[16,8,3]{0,1,2:T(8,128)}, u32[]{:S(2)}) copy-start(f32[16,8,3]{0,1,2:T(8,128)} %copy.345) | copy-start | bytes 4612
  696.4 62.6 %copy-start.25 = (f32[16,8,3]{0,1,2:T(8,128)S(1)}, f32[16,8,3]{0,1,2:T(8,128)}, u32[]{:S(2)}) copy-start(f32[16,8,3]{0,1,2:T(8,128)} %copy.305) | copy-start | bytes 4612
  893.3 13.6 %all-to-all-start.6 = ((bf16[32,1,4,1536]{3,2,1,0:T(4,128)(2,1)}), bf16[32,1,4,1536]{3,2,1,0:T(4,128)(2,1)S(1)}, u32[]{:S(2)}, u32[]{:S(2)}) async-start(bf16[32,1,4,1536]{3,2,1,0:T(4,128)(2,1)} %copy.375), calls=%async_computation.6 | async-start | bytes 786432 | tf_op jit(solution)/shard_map/all_to_all | solution.py:212
  (47 other events, 284.0 us)
Sparse Core Ops, SparseCore 0:
  796.9 73.4 all-reduce.6
